TPU v7x, 256 devices: a whole 4x4x8 slice. The times are simulated.
256 devices in a mesh: dp: 4 (over x), cls: 64 (over z, y, core).
Axes of the slice: x: 4, y: 4, z: 8, core: 2. Of those that a mesh axis runs over, the one named last changes fastest.
Arguments:
- embeddings: float32 [2048, 512], P('dp'), may hold values from -60 to 60, as said below
- classifier: float32 [1048576, 512], P(('dp', 'cls')), may hold values from -60 to 60, as said below
- labels: int32 [2048], replicated, may hold values from 0 to 1048575
- row_scale: float32 [2048], replicated, may hold values from 16 to 512
Outputs:
- loss: float32 [2048], P(('dp', 'cls'))
Inputs may be any that keep to these rules, and one draw needn't show every extreme that they name: `embeddings`: rows of different scales. `classifier`: rows of different scales.
All inputs are finite; a program needn't handle non-finite values.
Results may differ from a plain program's by a relative error of at most 0.0003.
Values sent between devices are 32-bit elements; how exact they have to be, the bound alone decides.
No kernel may reach another device: no remote copies, remote signals or barrier semaphores. Data moves between devices by JAX's collectives and lax.ppermute only.
A program may use at most 128 MiB of HBM per device.

v0:
```python
import math
import jax
import jax.numpy as jnp
from jax import lax
from jax.sharding import Mesh
from jax.sharding import PartitionSpec as P

DP_CLS = ("dp", "cls_0", "cls_1", "cls_2")
MARGIN = 0.5
COS_MARGIN = math.cos(MARGIN)
SIN_MARGIN = math.sin(MARGIN)


def gathered_once(shard, axis):
    leaves = jax.tree.leaves(shard)
    sequence = sorted(range(len(leaves)), key=lambda k: -leaves[k].size)
    width = (1, *leaves[sequence[0]].shape)[-1]
    lines = [
        jnp.pad(leaves[k].reshape(-1), (0, -leaves[k].size % width)).reshape(-1, width)
        for k in sequence
    ]
    both, at, found = (lax.all_gather(jnp.concatenate(lines), axis), 0, {})
    for k, line in zip(sequence, lines):
        section = both[:, at : at + len(line)].reshape(len(both), -1)
        found[k] = section[:, : leaves[k].size].reshape(-1, *leaves[k].shape)
        at += len(line)
    numbers = iter(range(len(leaves)))
    return jax.tree.map(lambda _: found[next(numbers)], shard)


def merged_by_axis(shard, axes, combine):
    for axis in axes:
        pieces = gathered_once(shard, axis)
        shard = jax.tree.map(lambda part: part[0], pieces)
        for k in range(1, lax.axis_size(axis)):
            shard = combine(shard, jax.tree.map(lambda part: part[k], pieces))
    return shard


def unit_rows(values):
    return values * lax.rsqrt(jnp.sum(values * values, axis=-1, keepdims=True) + 1e-06)


def margin_logit(units, picked, scales):
    cosine = jnp.sum(units * picked, axis=-1)
    across = units - cosine[:, None] * picked
    sine = jnp.sqrt(jnp.sum(across * across, axis=-1))
    return scales * (cosine * COS_MARGIN - sine * SIN_MARGIN)


def block_stats(units, rows, class_ids, labels, scales, picked, owned):
    cosine = lax.dot_general(
        units,
        rows,
        (((1,), (1,)), ((), ())),
        precision=lax.Precision.HIGHEST,
        preferred_element_type=jnp.float32,
    )
    target = margin_logit(units, picked, scales)
    hit = labels[:, None] == class_ids[None, :]
    logits = jnp.where(hit, target[:, None], scales[:, None] * cosine)
    peak = jnp.max(logits, axis=1)
    total = jnp.sum(jnp.exp(logits - peak[:, None]), axis=1)
    return (peak, total, jnp.where(owned, target, jnp.zeros_like(target)))


def merge_rows(first, second):
    peak = jnp.maximum(first[0], second[0])
    total = first[1] * jnp.exp(first[0] - peak) + second[1] * jnp.exp(second[0] - peak)
    return (peak, total, first[2] + second[2])


def body(embeddings, classifier, labels, row_scale):
    rows_here = classifier.shape[0]
    units_mine = unit_rows(embeddings)
    normed = unit_rows(classifier)
    offset = lax.axis_index(DP_CLS) * rows_here
    class_ids = offset + jnp.arange(rows_here, dtype=jnp.int32)
    owned_all = (labels >= offset) & (labels < offset + rows_here)
    local_all = jnp.clip(labels - offset, 0, rows_here - 1)
    count = labels.shape[0]
    picked = jnp.take(normed, local_all, axis=0)
    stats = block_stats(
        lax.all_gather(units_mine, "dp", axis=0, tiled=True),
        normed,
        class_ids,
        labels,
        row_scale,
        picked,
        owned_all,
    )
    peak, total, target = tuple((fresh for fresh in stats))
    share = count // lax.axis_size(DP_CLS)
    first = lax.axis_index(DP_CLS) * share
    peak, total, target = merged_by_axis((peak, total, target), DP_CLS, merge_rows)
    whole = peak + jnp.log(total) - target
    return lax.dynamic_slice_in_dim(whole, first, share)


def solution(mesh):
    torus = Mesh(mesh.devices.reshape(mesh.shape["dp"], 8, 4, 2), ("dp", "cls_0", "cls_1", "cls_2"))
    return jax.shard_map(
        body,
        mesh=torus,
        in_specs=(P("dp", None), P(DP_CLS, None), P(), P()),
        out_specs=P(DP_CLS),
        check_vma=False,
    )
```

profile of v0, /device:TPU:1, one launch (start us, length us, event | category | flops | bytes accessed | tf_op | source)
XLA Modules:
  0.0 210.5 jit_solution(7871280436764989805)
XLA Ops:
  6.5 1.4 multiply_reduce_fusion.3
  7.9 2.3 %broadcast_multiply_fusion.1 = f32[512,512]{1,0:T(8,128)} fusion(f32[512,512]{1,0:T(8,128)} %param.4, f32[512]{0:T(512)S(1)} %add_rsqrt_fusion.1), kind=kLoop, calls=%fused_computation.9 | loop fusion | flops 262144 | bytes 2099200 | tf_op jit(solution)/shard_map/mul | solution.py:41
  10.3 0.9 fusion.43
  11.2 4.1 %multiply_reduce_fusion = f32[4096]{0:T(1024)S(1)} fusion(f32[4096,512]{1,0:T(8,128)} %param.5), kind=kLoop, calls=%fused_computation.4 | loop fusion | flops 4190208 | bytes 8404992 | tf_op jit(solution)/shard_map/reduce_sum | solution.py:41
  15.3 0.8 copy-done.1
  16.1 3.6 %broadcast_multiply_fusion = f32[4096,512]{1,0:T(8,128)} fusion(f32[4096,512]{1,0:T(8,128)S(1)} %copy-done.1, f32[4096]{0:T(1024)S(1)} %add_rsqrt_fusion), kind=kLoop, calls=%fused_computation.7 | loop fusion | flops 2097152 | bytes 16793600 | tf_op jit(solution)/shard_map/mul | solution.py:41
  19.6 12.9 %gather_fusion = f32[2048,512]{1,0:T(8,128)} fusion(f32[4096,512]{1,0:T(8,128)} %broadcast_multiply_fusion, s32[2048]{0:T(1024)S(1)} %fusion.43), kind=kCustom, calls=%fused_computation | custom fusion | bytes 8396800 | tf_op jit(solution)/shard_map/jit(_take)/gather | solution.py:82
  32.6 32.2 %all-gather.10.cloned.1.call-done = f32[2048,512]{1,0:T(8,128)} async-done(((f32[512,512]{1,0:T(8,128)}), f32[2048,512]{1,0:T(8,128)}) %all-gather.10.cloned.1.call-update) | async-done | bytes 4194320 | tf_op jit(solution)/shard_map/all_gather | solution.py:84
  64.8 4.1 %multiply_reduce_fusion.2 = f32[2048]{0:T(1024)S(1)} fusion(f32[2048,512]{1,0:T(8,128)} %all-gather.10.cloned.1.call-done, f32[2048,512]{1,0:T(8,128)} %gather_fusion, pred[2048]{0:T(1024)(128)(4,1)S(1)} %compare_and_fusion), kind=kLoop, calls=%fused_computation.6 | loop fusion | flops 3143680 | bytes 8398848 | tf_op jit(solution)/shard_map/reduce_sum | solution.py:45
  68.9 0.6 copy-done
  69.5 3.6 %multiply_reduce_fusion.1 = f32[2048]{0:T(1024)S(1)} fusion(f32[2048,512]{1,0:T(8,128)} %all-gather.10.cloned.1.call-done, f32[2048,512]{1,0:T(8,128)S(1)} %copy-done, f32[2048]{0:T(1024)S(1)} %multiply_reduce_fusion.2, pred[2048]{0:T(1024)(128)(4,1)S(1)} %compare_and_fusion), kind=kLoop, calls=%fused_computation.5 | loop fusion | flops 5240832 | bytes 8407040 | tf_op jit(solution)/shard_map/reduce_sum | solution.py:47
  73.1 0.1 copy-done.2
  73.2 1.4 slice-done.1
  74.7 59.6 %fusion = (f32[2048]{0:T(1024)S(1)}, f32[2048,4096]{1,0:T(8,128)}) fusion(f32[2048]{0:T(1024)S(1)} %copy-done.4, f32[2048]{0:T(1024)S(1)} %get-tuple-element.14, s32[4096]{0:T(1024)S(1)} %iota_add_fusion, s32[2048]{0:T(1024)S(1)} %copy-done.3, f32[2048,512]{1,0:T(8,128)S(1)} %copy-done.2, f32[4096,512]{1,0:T(8,128)S(1)} %bitcast.325), kind=kOutput, calls=%fused_computation.3 | convolution fusion | flops 51573161984 | bytes 46186496 | tf_op jit(solution)/shard_map/dot_general | solution.py:52
  134.3 15.2 %exponential_reduce_fusion = f32[2048]{0:T(1024)S(1)} fusion(f32[2048,4096]{1,0:T(8,128)} %get-tuple-element.21, f32[2048]{0:T(1024)S(1)} %get-tuple-element.20, f32[2048]{0:T(1024)S(1)} %copy-done.4, f32[2048]{0:T(1024)S(1)} %get-tuple-element.14, s32[4096]{0:T(1024)S(1)} %iota_add_fusion, s32[2048]{0:T(1024)S(1)} %copy-done.3), kind=kLoop, calls=%fused_computation.1 | loop fusion | flops 41940992 | bytes 33611776 | tf_op jit(solution)/shard_map/reduce_sum | solution.py:63
  149.5 9.1 %all-gather.4 = f32[4,3,2048]{2,1,0:T(4,128)S(1)} all-gather(f32[1,3,2048]{2,1,0:T(4,128)S(1)} %maximum_bitcast_fusion), channel_id=2, replica_groups=mesh['dp'=4,'cls_0'=8,'cls_1'=4,'cls_2'=2] {'dp'}, dimensions={0}, use_global_device_ids=true | all-gather | bytes 122880 | tf_op jit(solution)/shard_map/all_gather | solution.py:22
  158.6 0.1 fusion.35
  158.7 20.3 %all-gather.5 = f32[8,3,2048]{2,1,0:T(4,128)S(1)} all-gather(f32[1,3,2048]{2,1,0:T(4,128)S(1)} %maximum_bitcast_fusion.1), channel_id=3, replica_groups=mesh['dp'=4,'cls_0'=8,'cls_1'=4,'cls_2'=2] {'cls_0'}, dimensions={0}, use_global_device_ids=true | all-gather | bytes 221184 | tf_op jit(solution)/shard_map/all_gather | solution.py:22
  179.0 0.1 fusion.11
  179.1 0.2 fusion.13
  179.3 9.7 %all-gather.6 = f32[4,3,2048]{2,1,0:T(4,128)S(1)} all-gather(f32[1,3,2048]{2,1,0:T(4,128)S(1)} %maximum_bitcast_fusion.2), channel_id=4, replica_groups=mesh['dp'=4,'cls_0'=8,'cls_1'=4,'cls_2'=2] {'cls_1'}, dimensions={0}, use_global_device_ids=true | all-gather | bytes 122880 | tf_op jit(solution)/shard_map/all_gather | solution.py:22
  189.1 0.1 fusion.3
  189.2 13.8 %all-gather.7 = f32[2,3,2048]{2,1,0:T(4,128)S(1)} all-gather(f32[1,3,2048]{2,1,0:T(4,128)S(1)} %maximum_bitcast_fusion.3), channel_id=5, replica_groups=mesh['dp'=4,'cls_0'=8,'cls_1'=4,'cls_2'=2] {'cls_2'}, dimensions={0}, use_global_device_ids=true | all-gather | bytes 73728 | tf_op jit(solution)/shard_map/all_gather | solution.py:22
  203.1 0.6 dynamic-slice_subtract_fusion
  (27 shorter events, 0.3 us)
Async XLA Ops:
  6.5 58.3 %all-gather.10.cloned.1.call-start = ((), (), s32[]{:S(2)}) async-start(), calls=%async_computation | async-start | bytes 5242880 | tf_op jit(solution)/shard_map/all_gather | solution.py:84
  10.3 5.8 %copy-start.1 = (f32[4096,512]{1,0:T(8,128)S(1)}, f32[4096,512]{1,0:T(8,128)}, u32[]{:S(2)}) copy-start(f32[4096,512]{1,0:T(8,128)} %param.5) | copy-start | bytes 25165828
  19.6 13.0 %copy-start.3 = (s32[2048]{0:T(1024)S(1)}, s32[2048]{0:T(1024)}, u32[]{:S(2)}) copy-start(s32[2048]{0:T(1024)} %param.6) | copy-start | bytes 24580
  32.6 40.5 %copy-start.4 = (f32[2048]{0:T(1024)S(1)}, f32[2048]{0:T(1024)}, u32[]{:S(2)}) copy-start(f32[2048]{0:T(1024)} %param.7) | copy-start | bytes 24580
  64.8 4.7 %copy-start = (f32[2048,512]{1,0:T(8,128)S(1)}, f32[2048,512]{1,0:T(8,128)}, u32[]{:S(2)}) copy-start(f32[2048,512]{1,0:T(8,128)} %gather_fusion) | copy-start | bytes 12582916
  64.8 8.3 %slice-start = ((s8[8388608]{0:T(1024)(128)(4,1)}), s8[4194304]{0:T(1024)(128)(4,1)S(1)}, s32[]{:S(2)}) async-start(s8[8388608]{0:T(1024)(128)(4,1)} %bitcast.324), calls=%async_computation.1 | async-start | bytes 8388608
  64.8 8.4 %copy-start.2 = (f32[2048,512]{1,0:T(8,128)S(1)}, f32[2048,512]{1,0:T(8,128)}, u32[]{:S(2)}) copy-start(f32[2048,512]{1,0:T(8,128)} %all-gather.10.cloned.1.call-done) | copy-start | bytes 12582916
  69.5 5.2 %slice-start.1 = ((s8[8388608]{0:T(1024)(128)(4,1)}), s8[4194304]{0:T(1024)(128)(4,1)S(1)}, s32[]{:S(2)}) async-start(s8[8388608]{0:T(1024)(128)(4,1)} %bitcast.324), calls=%async_computation.2 | async-start | bytes 8388608
Sparse Core Ops, SparseCore 0:
  10.4 54.3 all-gather.9
where the time goes:
time: 211 us
  matrix products  59.6 us (28%)
  blocking collectives  52.9 us (25%)
  other arithmetic  36.4 us (17%)
  waiting for transfers between devices  32.2 us (15%)
  local copies, waits for them, and re-layouts  15.8 us (7%)
  between operations  13.6 us (6%)
    dot_general x1, matrix products, block_stats(): lax.dot_general(units, rows, (((1,), (1,)), ((), ())), precision=lax.Prec...  59.6 us
    all_gather x4, blocking collectives, gathered_once(): both, at, found = (lax.all_gather(jnp.concatenate(lines), axis), 0, {})  52.9 us
    all_gather x1, waiting for transfers between devices, body(): lax.all_gather(units_mine, 'dp', axis=0, tiled=True)  32.2 us
    reduce_sum x1, other arithmetic, block_stats(): total = jnp.sum(jnp.exp(logits - peak[:, None]), axis=1)  15.2 us
    gather x1, local copies, waits for them, and re-layouts, body(): picked = jnp.take(normed, local_all, axis=0)  12.9 us
    mul x2, other arithmetic, unit_rows(): values * lax.rsqrt(jnp.sum(values * values, axis=-1, keepdims=True) + 1e-06)  5.9 us
    reduce_sum x2, other arithmetic, unit_rows(): jnp.sum(values * values, axis=-1, keepdims=True) + 1e-06  5.52 us
  transfers between devices with their start and end apart: 1, of which 1 were waited for; matrix products, arithmetic and copies ran while one was open for 10% of the time, Pallas kernels for 0%

commit v1 on v0

--- a/solution.py
+++ b/solution.py
@@ -9,6 +9,14 @@
 MARGIN = 0.5
 COS_MARGIN = math.cos(MARGIN)
 SIN_MARGIN = math.sin(MARGIN)
+
+
+def tiled_gather(shard, axis, dim):
+    count = lax.axis_size(axis)
+    repeats = [count if d == dim else 1 for d in range(shard.ndim)]
+    return lax.all_to_all(
+        jnp.tile(shard, repeats), axis, split_axis=dim, concat_axis=dim, tiled=True
+    )
 
 
 def gathered_once(shard, axis):
@@ -81,13 +89,7 @@
     count = labels.shape[0]
     picked = jnp.take(normed, local_all, axis=0)
     stats = block_stats(
-        lax.all_gather(units_mine, "dp", axis=0, tiled=True),
-        normed,
-        class_ids,
-        labels,
-        row_scale,
-        picked,
-        owned_all,
+        tiled_gather(units_mine, "dp", 0), normed, class_ids, labels, row_scale, picked, owned_all
     )
     peak, total, target = tuple((fresh for fresh in stats))
     share = count // lax.axis_size(DP_CLS)

time: 211 us -> 202 us (0.957)
  between operations: 13.6 us -> 0.19 us
  waiting for transfers between devices: 32.2 us -> 24.1 us
  blocking collectives: 52.9 us -> 58.2 us
  starting transfers between devices: 0.01 us -> 4.85 us
    all_gather x1 -> x0, waiting for transfers between devices: 32.2 us -> none  [body(): lax.all_gather(units_mine, 'dp', axis=0, tiled=True)]
    all_to_all x0 -> x1, waiting for transfers between devices: none -> 24.1 us  [tiled_gather(): lax.all_to_all(jnp.tile(shard, repeats), axis, split_axis=dim, concat_axi...]
    all_gather x4, blocking collectives: 52.9 us -> 58.2 us  [gathered_once(): both, at, found = (lax.all_gather(jnp.concatenate(lines), axis), 0, {})]
    all_to_all x0 -> x1, starting transfers between devices: none -> 4.85 us  [tiled_gather(): lax.all_to_all(jnp.tile(shard, repeats), axis, split_axis=dim, concat_axi...]
    another operation x0 -> x1, local copies, waits for them, and re-layouts: none -> 2.51 us  [tiled_gather(): jnp.tile(shard, repeats)]
  transfers between devices with their start and end apart: 1 -> 1, of which waited for: 1 -> 1; matrix products, arithmetic and copies ran while one was open for 10% -> 11% of each run, Pallas kernels for 0% -> 0%
where the time goes in v1:
time: 202 us
  matrix products  61.1 us (30%)
  blocking collectives  58.2 us (29%)
  other arithmetic  36.2 us (18%)
  waiting for transfers between devices  24.1 us (12%)
  local copies, waits for them, and re-layouts  16.8 us (8%)
  starting transfers between devices  4.85 us (2%)
    dot_general x1, matrix products, block_stats(): lax.dot_general(units, rows, (((1,), (1,)), ((), ())), precision=lax.Prec...  61.1 us
    all_gather x4, blocking collectives, gathered_once(): both, at, found = (lax.all_gather(jnp.concatenate(lines), axis), 0, {})  58.2 us
    all_to_all x1, waiting for transfers between devices, tiled_gather(): lax.all_to_all(jnp.tile(shard, repeats), axis, split_axis=dim, concat_axi...  24.1 us
    reduce_sum x1, other arithmetic, block_stats(): total = jnp.sum(jnp.exp(logits - peak[:, None]), axis=1)  15.2 us
    gather x1, local copies, waits for them, and re-layouts, body(): picked = jnp.take(normed, local_all, axis=0)  12.9 us
    mul x2, other arithmetic, unit_rows(): values * lax.rsqrt(jnp.sum(values * values, axis=-1, keepdims=True) + 1e-06)  7.15 us
    reduce_sum x2, other arithmetic, unit_rows(): jnp.sum(values * values, axis=-1, keepdims=True) + 1e-06  5.4 us
    all_to_all x1, starting transfers between devices, tiled_gather(): lax.all_to_all(jnp.tile(shard, repeats), axis, split_axis=dim, concat_axi...  4.85 us
  transfers between devices with their start and end apart: 1, of which 1 were waited for; matrix products, arithmetic and copies ran while one was open for 11% of the time, Pallas kernels for 0%

profile of v1, /device:TPU:1, one launch (start us, length us, event | category | flops | bytes accessed | tf_op | source)
XLA Modules:
  0.0 201.6 jit_solution(16188554033315869577)
XLA Ops:
  0.0 1.4 multiply_reduce_fusion.3
  1.4 1.4 broadcast_multiply_fusion.1
  2.8 2.5 %tile.2 = f32[4,512,512]{2,1,0:T(8,128)} broadcast(f32[512,512]{1,0:T(8,128)S(1)} %broadcast_multiply_fusion.1), dimensions={1,2} | broadcast | bytes 5242880 | tf_op jit(solution)/shard_map/tile | solution.py:18
  5.3 4.9 %all-to-all-start = ((f32[4,512,512]{2,1,0:T(8,128)}), f32[4,512,512]{2,1,0:T(8,128)}, u32[]{:S(2)}, u32[]{:S(2)}) async-start(f32[4,512,512]{2,1,0:T(8,128)} %tile.2), calls=%async_computation | async-start | bytes 8388608 | tf_op jit(solution)/shard_map/all_to_all | solution.py:17
  10.1 0.0 copy-done.1
  10.2 4.0 %multiply_reduce_fusion = f32[4096]{0:T(1024)S(1)} fusion(f32[4096,512]{1,0:T(8,128)} %param.5), kind=kLoop, calls=%fused_computation.4 | loop fusion | flops 4190208 | bytes 8404992 | tf_op jit(solution)/shard_map/reduce_sum | solution.py:49
  14.2 5.8 %broadcast_multiply_fusion = f32[4096,512]{1,0:T(8,128)} fusion(f32[4096,512]{1,0:T(8,128)} %param.5, f32[4096]{0:T(1024)S(1)} %add_rsqrt_fusion), kind=kLoop, calls=%fused_computation.7 | loop fusion | flops 2097152 | bytes 16793600 | tf_op jit(solution)/shard_map/mul | solution.py:49
  20.0 12.9 %gather_fusion = f32[2048,512]{1,0:T(8,128)} fusion(f32[4096,512]{1,0:T(8,128)} %broadcast_multiply_fusion, s32[2048]{0:T(1024)S(1)} %fusion.43), kind=kCustom, calls=%fused_computation | custom fusion | bytes 8396800 | tf_op jit(solution)/shard_map/jit(_take)/gather | solution.py:90
  32.9 24.1 %all-to-all-done = f32[4,512,512]{2,1,0:T(8,128)} async-done(((f32[4,512,512]{2,1,0:T(8,128)}), f32[4,512,512]{2,1,0:T(8,128)}, u32[]{:S(2)}, u32[]{:S(2)}) %all-to-all-start) | async-done | bytes 4194336 | tf_op jit(solution)/shard_map/all_to_all | solution.py:17
  57.1 4.0 %multiply_reduce_fusion.2 = f32[4,512]{1,0:T(4,128)S(1)} fusion(f32[4,512,512]{2,1,0:T(8,128)} %all-to-all-done, f32[4,512,512]{2,1,0:T(8,128)} %bitcast.331, pred[4,512]{1,0:T(4,128)(4,1)S(1)} %broadcast_in_dim.33), kind=kLoop, calls=%fused_computation.6 | loop fusion | flops 3143680 | bytes 8398848 | tf_op jit(solution)/shard_map/reduce_sum | solution.py:53
  61.1 0.6 copy-done
  61.7 3.1 %multiply_reduce_fusion.1 = f32[4,512]{1,0:T(4,128)S(1)} fusion(f32[4,512,512]{2,1,0:T(8,128)} %all-to-all-done, f32[4,512,512]{2,1,0:T(8,128)S(1)} %bitcast.332, f32[4,512]{1,0:T(4,128)S(1)} %multiply_reduce_fusion.2, pred[4,512]{1,0:T(4,128)(4,1)S(1)} %broadcast_in_dim.33), kind=kLoop, calls=%fused_computation.5 | loop fusion | flops 5240832 | bytes 8407040 | tf_op jit(solution)/shard_map/reduce_sum | solution.py:55
  64.9 0.8 slice-done.1
  65.7 61.1 %fusion = (f32[2048]{0:T(1024)S(1)}, f32[2048,4096]{1,0:T(8,128)}) fusion(f32[2048]{0:T(1024)S(1)} %copy-done.2, f32[2048]{0:T(1024)S(1)} %get-tuple-element.14, s32[4096]{0:T(1024)S(1)} %iota_add_fusion, s32[2048]{0:T(1024)S(1)} %copy-done.1, f32[2048,512]{1,0:T(8,128)} %bitcast.1, f32[4096,512]{1,0:T(8,128)S(1)} %bitcast.330), kind=kOutput, calls=%fused_computation.3 | convolution fusion | flops 51573161984 | bytes 46186496 | tf_op jit(solution)/shard_map/dot_general | solution.py:60
  126.8 15.2 %exponential_reduce_fusion = f32[2048]{0:T(1024)S(1)} fusion(f32[2048,4096]{1,0:T(8,128)} %get-tuple-element.21, f32[2048]{0:T(1024)S(1)} %get-tuple-element.20, f32[2048]{0:T(1024)S(1)} %copy-done.2, f32[2048]{0:T(1024)S(1)} %get-tuple-element.14, s32[4096]{0:T(1024)S(1)} %iota_add_fusion, s32[2048]{0:T(1024)S(1)} %copy-done.1), kind=kLoop, calls=%fused_computation.1 | loop fusion | flops 41940992 | bytes 33611776 | tf_op jit(solution)/shard_map/reduce_sum | solution.py:71
  142.0 9.1 %all-gather.4 = f32[4,3,2048]{2,1,0:T(4,128)S(1)} all-gather(f32[1,3,2048]{2,1,0:T(4,128)S(1)} %maximum_bitcast_fusion), channel_id=2, replica_groups=mesh['dp'=4,'cls_0'=8,'cls_1'=4,'cls_2'=2] {'dp'}, dimensions={0}, use_global_device_ids=true | all-gather | bytes 122880 | tf_op jit(solution)/shard_map/all_gather | solution.py:30
  151.2 0.1 fusion.35
  151.3 25.0 %all-gather.5 = f32[8,3,2048]{2,1,0:T(4,128)S(1)} all-gather(f32[1,3,2048]{2,1,0:T(4,128)S(1)} %maximum_bitcast_fusion.1), channel_id=3, replica_groups=mesh['dp'=4,'cls_0'=8,'cls_1'=4,'cls_2'=2] {'cls_0'}, dimensions={0}, use_global_device_ids=true | all-gather | bytes 221184 | tf_op jit(solution)/shard_map/all_gather | solution.py:30
  176.3 0.1 fusion.11
  176.4 0.2 fusion.13
  176.6 9.6 %all-gather.6 = f32[4,3,2048]{2,1,0:T(4,128)S(1)} all-gather(f32[1,3,2048]{2,1,0:T(4,128)S(1)} %maximum_bitcast_fusion.2), channel_id=4, replica_groups=mesh['dp'=4,'cls_0'=8,'cls_1'=4,'cls_2'=2] {'cls_1'}, dimensions={0}, use_global_device_ids=true | all-gather | bytes 122880 | tf_op jit(solution)/shard_map/all_gather | solution.py:30
  186.3 0.1 fusion.3
  186.4 14.5 %all-gather.7 = f32[2,3,2048]{2,1,0:T(4,128)S(1)} all-gather(f32[1,3,2048]{2,1,0:T(4,128)S(1)} %maximum_bitcast_fusion.3), channel_id=5, replica_groups=mesh['dp'=4,'cls_0'=8,'cls_1'=4,'cls_2'=2] {'cls_2'}, dimensions={0}, use_global_device_ids=true | all-gather | bytes 73728 | tf_op jit(solution)/shard_map/all_gather | solution.py:30
  201.0 0.6 dynamic-slice_subtract_fusion
  (26 shorter events, 0.3 us)
Async XLA Ops:
  0.0 10.1 %copy-start.1 = (s32[2048]{0:T(1024)S(1)}, s32[2048]{0:T(1024)}, u32[]{:S(2)}) copy-start(s32[2048]{0:T(1024)} %param.6) | copy-start | bytes 24580
  5.3 51.8 %all-to-all-start = ((f32[4,512,512]{2,1,0:T(8,128)}), f32[4,512,512]{2,1,0:T(8,128)}, u32[]{:S(2)}, u32[]{:S(2)}) async-start(f32[4,512,512]{2,1,0:T(8,128)} %tile.2), calls=%async_computation | async-start | bytes 8388608 | tf_op jit(solution)/shard_map/all_to_all | solution.py:17
  57.1 4.7 %copy-start = (f32[2048,512]{1,0:T(8,128)S(1)}, f32[2048,512]{1,0:T(8,128)}, u32[]{:S(2)}) copy-start(f32[2048,512]{1,0:T(8,128)} %gather_fusion) | copy-start | bytes 12582916
  57.1 7.8 %copy-start.2 = (f32[2048]{0:T(1024)S(1)}, f32[2048]{0:T(1024)}, u32[]{:S(2)}) copy-start(f32[2048]{0:T(1024)} %param.7) | copy-start | bytes 24580
  57.1 7.8 %slice-start = ((s8[8388608]{0:T(1024)(128)(4,1)}), s8[4194304]{0:T(1024)(128)(4,1)S(1)}, s32[]{:S(2)}) async-start(s8[8388608]{0:T(1024)(128)(4,1)} %bitcast.329), calls=%async_computation.1 | async-start | bytes 8388608
  61.7 4.0 %slice-start.1 = ((s8[8388608]{0:T(1024)(128)(4,1)}), s8[4194304]{0:T(1024)(128)(4,1)S(1)}, s32[]{:S(2)}) async-start(s8[8388608]{0:T(1024)(128)(4,1)} %bitcast.329), calls=%async_computation.2 | async-start | bytes 8388608
